TPU v7x, 256 devices: a whole 4x4x8 slice. The times are simulated.
256 devices in a mesh: row: 16 (over z, core), col: 16 (over y, x).
Axes of the slice: x: 4, y: 4, z: 8, core: 2. Of those that a mesh axis runs over, the one named last changes fastest.
Arguments:
- inputs: bfloat16 [2048, 8192], P('col', 'row'), may hold values from -6 to 6
- weight: bfloat16 [8192, 28672], P('row', 'col'), may hold values from -0.09375 to 0.09375
- mask: int32 [64, 224], P('row', 'col'), may hold values 0 or 1
- cotangent: bfloat16 [2048, 28672], P('row', 'col'), may hold values from -6 to 6
Outputs:
- outputs: bfloat16 [2048, 28672], P('row', 'col')
- input_grad: bfloat16 [2048, 8192], P('col', 'row')
- weight_grad: bfloat16 [8192, 28672], P('row', 'col')
Inputs may be any that keep to these rules, and one draw needn't show every extreme that they name: mask holds only zeros and ones.
All inputs are finite; a program needn't handle non-finite values. No bound on the sum of `mask` on one device may be relied on, other than what follows from the above.
Results may differ from a plain program's by a relative error of at most 0.022.
Values may be sent and summed in bfloat16 or wider, within the bound.
A program may use at most 128 MiB of HBM per device.

v0:
```python
import jax
import jax.numpy as jnp
from jax import lax
from jax.sharding import PartitionSpec as P

BLOCK = 128


def expand_mask(mask_tile):
    tile_rows, tile_cols = mask_tile.shape
    mask_bf16 = mask_tile.astype(jnp.bfloat16)
    widened = jnp.broadcast_to(mask_bf16[:, None, :, None], (tile_rows, BLOCK, tile_cols, BLOCK))
    return widened.reshape(tile_rows * BLOCK, tile_cols * BLOCK)


def local(inputs, weight, mask, cotangent):
    keep_mask = expand_mask(mask)
    masked = weight * keep_mask
    whole = lax.all_gather(inputs, "col", axis=0, tiled=True)
    token_total = whole.shape[0]
    chosen = whole
    outputs = lax.psum_scatter(
        jnp.dot(chosen, masked, preferred_element_type=jnp.float32).astype(jnp.bfloat16),
        "row",
        scatter_dimension=0,
        tiled=True,
    )
    shard_rows = lax.all_gather(cotangent, "row", axis=0, tiled=True)
    partial_value = lax.dot_general(
        shard_rows, masked, (((1,), (1,)), ((), ())), preferred_element_type=jnp.float32
    )
    grad_parts = partial_value.astype(jnp.bfloat16)
    chosen = whole
    weight_acc = lax.dot_general(
        chosen, shard_rows, (((0,), (0,)), ((), ())), preferred_element_type=jnp.float32
    )
    grad_parts, weight_acc = (grad_parts, weight_acc)
    summed = lax.psum_scatter(
        grad_parts.astype(jnp.float32).astype(jnp.bfloat16), "col", scatter_dimension=0, tiled=True
    )
    grad_scale = token_total ** (-0.5)
    weight_grad = (weight_acc * keep_mask.astype(jnp.float32) * grad_scale).astype(jnp.bfloat16)
    return (outputs, summed, weight_grad)


def solution(mesh):
    placed = (P("col", "row"), P("row", "col"), P("row", "col"), P("row", "col"))
    return jax.shard_map(
        local,
        mesh=mesh,
        in_specs=placed,
        out_specs=(P("row", "col"), P("col", "row"), P("row", "col")),
        check_vma=False,
    )
```

profile of v0, /device:TPU:1, one launch (start us, length us, event | category | flops | bytes accessed | tf_op | source)
XLA Modules:
  0.0 273.2 jit_solution(2744342380747078628)
XLA Ops:
  7.2 0.0 all-gather.5.cloned.1.call-start
  7.2 0.7 all-gather.5.cloned.1.call-update
  7.9 0.0 all-gather.3.cloned.1.call-start
  7.9 0.7 all-gather.3.cloned.1.call-update
  8.6 0.0 reduce-scatter.9.cloned.1.call-start
  8.7 0.7 convert_element_type.23
  9.4 0.1 copy.14
  9.5 3.8 %copy.15 = bf16[512,1792]{0,1:T(8,128)(2,1)} copy(bf16[512,1792]{1,0:T(8,128)(2,1)} %param.5) | data formatting | bytes 3670016 | tf_op args[1]
  13.3 51.7 %all-gather.5.cloned.1.call-done = bf16[2048,1792]{1,0:T(8,128)(2,1)} async-done(((bf16[128,1792]{1,0:T(8,128)(2,1)}), bf16[2048,1792]{1,0:T(8,128)(2,1)}) %all-gather.5.cloned.1.call-update) | async-done | bytes 7340048 | tf_op jit(solution)/shard_map/all_gather | solution.py:28
  65.1 0.5 broadcast_in_dim.2
  65.6 9.1 %fusion.1 = bf16[2048,512]{0,1:T(8,128)(2,1)} fusion(bf16[2048,1792]{1,0:T(8,128)(2,1)} %all-gather.5.cloned.1.call-done, bf16[512,1792]{0,1:T(8,128)(2,1)} %copy.15, bf16[224,8,4,128]{3,2,1,0:T(4,128)(2,1)S(1)} %bitcast.23), kind=kOutput, calls=%fused_computation.4 | convolution fusion | flops 3760062464 | bytes 13107200 | tf_op jit(solution)/shard_map/dot_general | solution.py:29
  74.7 4.0 %copy.21 = bf16[2048,512]{1,0:T(8,128)(2,1)} copy(bf16[2048,512]{0,1:T(8,128)(2,1)} %fusion.1) | data formatting | bytes 4194304
  78.6 0.0 reduce-scatter.9.cloned.1.call-update
  78.6 0.2 reduce-scatter.7.cloned.1.call-start
  78.9 35.9 %all-gather.3.cloned.1.call-done = bf16[2048,512]{1,0:T(8,128)(2,1)} async-done(((bf16[128,512]{1,0:T(8,128)(2,1)}), bf16[2048,512]{1,0:T(8,128)(2,1)}) %all-gather.3.cloned.1.call-update) | async-done | bytes 2097168 | tf_op jit(solution)/shard_map/all_gather | solution.py:19
  114.8 9.1 %fusion = bf16[2048,1792]{0,1:T(8,128)(2,1)} fusion(bf16[2048,512]{1,0:T(8,128)(2,1)} %all-gather.3.cloned.1.call-done, bf16[512,1792]{0,1:T(8,128)(2,1)} %copy.15, bf16[224,8,4,128]{3,2,1,0:T(4,128)(2,1)S(1)} %bitcast.24), kind=kOutput, calls=%fused_computation.1 | convolution fusion | flops 3762683904 | bytes 13107200 | tf_op jit(solution)/shard_map/dot_general | solution.py:23
  123.9 10.1 %copy.19 = bf16[2048,1792]{1,0:T(8,128)(2,1)} copy(bf16[2048,1792]{0,1:T(8,128)(2,1)} %fusion) | data formatting | bytes 14680064
  134.0 0.0 reduce-scatter.7.cloned.1.call-update
  134.0 1.5 copy.31
  135.5 2.8 %copy.16 = bf16[512,1792]{1,0:T(8,128)(2,1)S(1)} copy(bf16[512,1792]{0,1:T(8,128)(2,1)} %bitcast.26) | data formatting | bytes 3670016 | tf_op jit(solution)/shard_map/reshape | solution.py:13
  138.3 9.1 %multiply_convert_fusion = bf16[512,1792]{1,0:T(8,128)(2,1)} fusion(bf16[512,1792]{1,0:T(8,128)(2,1)S(1)} %copy.16, bf16[2048,512]{1,0:T(8,128)(2,1)} %all-gather.3.cloned.1.call-done, bf16[2048,1792]{1,0:T(8,128)(2,1)} %all-gather.5.cloned.1.call-done), kind=kOutput, calls=%fused_computation.2 | convolution fusion | flops 3761766400 | bytes 13107200 | tf_op jit(solution)/shard_map/dot_general | solution.py:34
  147.5 49.4 %reduce-scatter.9.cloned.1.call-done = bf16[128,512]{1,0:T(8,128)(2,1)} async-done(((bf16[2048,512]{1,0:T(8,128)(2,1)}), bf16[128,512]{1,0:T(8,128)(2,1)}) %reduce-scatter.9.cloned.1.call-update) | async-done | bytes 131088
  196.9 69.7 %reduce-scatter.7.cloned.1.call-done = bf16[128,1792]{1,0:T(8,128)(2,1)} async-done(((bf16[2048,1792]{1,0:T(8,128)(2,1)}), bf16[128,1792]{1,0:T(8,128)(2,1)}) %reduce-scatter.7.cloned.1.call-update) | async-done | bytes 458768
Async XLA Ops:
  7.2 57.9 %all-gather.5.cloned.1.call-start = ((), (), s32[]{:S(2)}) async-start(), calls=%async_computation.3 | async-start | bytes 7798784 | tf_op jit(solution)/shard_map/all_gather | solution.py:28
  7.9 106.9 %all-gather.3.cloned.1.call-start = ((), (), s32[]{:S(2)}) async-start(), calls=%async_computation.2 | async-start | bytes 2228224 | tf_op jit(solution)/shard_map/all_gather | solution.py:19
  8.6 188.2 %reduce-scatter.9.cloned.1.call-start = ((), (), s32[]{:S(2)}) async-start(), calls=%async_computation.5 | async-start | bytes 2228224
  78.6 188.0 %reduce-scatter.7.cloned.1.call-start = ((), (), s32[]{:S(2)}) async-start(), calls=%async_computation.4 | async-start | bytes 7798784
Sparse Core Ops, SparseCore 0:
  9.8 55.1 all-gather.4
  67.5 47.2 all-gather.2
  118.9 77.9 reduce-scatter.8
  200.0 66.5 reduce-scatter.6
where the time goes:
time: 276 us; the launch traced here: 273 us
  waiting for transfers between devices  208 us (75%)
  matrix products  27.3 us (10%)
  local copies, waits for them, and re-layouts  22.8 us (8%)
  between operations  13.8 us (5%)
    unnamed x6, waiting for transfers between devices  121 us
    all_gather x1, waiting for transfers between devices, local(): shard_rows = lax.all_gather(cotangent, 'row', axis=0, tiled=True)  51.7 us
    all_gather x1, waiting for transfers between devices, local(): whole = lax.all_gather(inputs, 'col', axis=0, tiled=True)  35.9 us
    unnamed x4, local copies, waits for them, and re-layouts  19.4 us
    dot_general x1, matrix products, local(): lax.dot_general(chosen, shard_rows, (((0,), (0,)), ((), ())), preferred_e...  9.14 us
    dot_general x1, matrix products, local(): jnp.dot(chosen, masked, preferred_element_type=jnp.float32)  9.1 us
    dot_general x1, matrix products, local(): lax.dot_general(shard_rows, masked, (((1,), (1,)), ((), ())), preferred_e...  9.06 us
  transfers between devices with their start and end apart: 4, of which 4 were waited for; matrix products, arithmetic and copies ran while one was open for 19% of the time, Pallas kernels for 0%

commit v1 on v0

v1 whole, which is shorter than its diff:
```python
import functools

import jax
import jax.numpy as jnp
from jax import lax
from jax.experimental import pallas as pl
from jax.experimental.pallas import tpu as pltpu
from jax.sharding import PartitionSpec as P

BLOCK = 128
NZ = 8
NC = 16
F32 = jnp.float32
BF16 = jnp.bfloat16
UP, DOWN = 0, 1


def remote(src, dst, send_sem, recv_sem, device):
    return pltpu.make_async_remote_copy(
        src_ref=src,
        dst_ref=dst,
        send_sem=send_sem,
        recv_sem=recv_sem,
        device_id=device,
        device_id_type=pl.DeviceIdType.MESH,
    )


def kernel(
    scale,
    x_hbm, w_hbm, mask_smem, c_hbm,
    out_hbm, ig_hbm, wg_hbm,
    X, XT, W, WT, C, PO, PS_out, PS, S, R, G, GR, WG, OUT, IG,
    load_sem, x_send, x_recv, az_send, az_recv, as_send, as_recv,
    ps_send, ps_recv, r_send, r_recv, g_send, g_recv, store_sem,
):
    row = lax.axis_index("row")
    col = lax.axis_index("col")
    z, core = row // 2, row % 2
    tok, width = c_hbm.shape
    depth = x_hbm.shape[1]
    half = tok // 2
    up = ((row + 2) % (2 * NZ), col)
    down = ((row + 2 * NZ - 2) % (2 * NZ), col)
    sibling = (row + 1 - 2 * core, col)
    toward = (up, down)
    my_rows = core * tok

    def partner(j):
        xx, yy = col % 4, col // 4
        return ((yy + j // 4) % 4) * 4 + (xx + j % 4) % 4

    def sender(j):
        xx, yy = col % 4, col // 4
        return ((yy + 4 - j // 4) % 4) * 4 + (xx + 4 - j % 4) % 4

    load_c = pltpu.make_async_copy(c_hbm, C.at[pl.ds(my_rows, tok)], load_sem.at[0])
    load_x = pltpu.make_async_copy(x_hbm, X.at[col], load_sem.at[1])
    load_w = pltpu.make_async_copy(w_hbm, W, load_sem.at[2])
    load_c.start()
    load_x.start()
    load_w.start()

    barrier = pltpu.get_barrier_semaphore()
    for device in (up, down, sibling):
        pl.semaphore_signal(barrier, inc=1, device_id=device, device_id_type=pl.DeviceIdType.MESH)

    def greet(j, carry):
        pl.semaphore_signal(barrier, inc=1, device_id=(row, partner(j)), device_id_type=pl.DeviceIdType.MESH)
        return carry

    lax.fori_loop(1, NC, greet, 0)
    pl.semaphore_wait(barrier, NC + 2)

    def chunk(rel, part, owner=core):
        return C.at[pl.ds(rel * 2 * tok + owner * tok + part * half, half)]

    def gather_copy(way, part, dist):
        rel = (-dist if way == UP else dist) % NZ
        land = (rel - 1 if way == UP else rel + 1) % NZ
        return remote(chunk(rel, part), chunk(land, part), az_send.at[way, part, dist], az_recv.at[way, part, dist], toward[way])

    def share_copy(rel, part):
        return remote(chunk(rel, part), chunk(rel, part), as_send.at[rel, part], as_recv.at[rel, part], sibling)

    def share_wait(rel):
        for part in range(2):
            other = chunk(rel, part, 1 - core)
            remote(other, other, as_send.at[rel, part], as_recv.at[rel, part], sibling).wait_recv()

    def last(way, part):
        return NZ // 2 if part == way else NZ // 2 - 1

    load_c.wait()
    for part in range(2):
        for way in (UP, DOWN):
            gather_copy(way, part, 0).start()
    for part in range(2):
        share_copy(0, part).start()
    load_x.wait()

    def x_copy(j):
        return remote(X.at[col], X.at[col], x_send.at[j], x_recv.at[j], (row, partner(j)))

    def x_start(j, carry):
        x_copy(j).start()
        return carry

    lax.fori_loop(1, NC, x_start, 0)

    def x_wait(j, carry):
        land = X.at[sender(j)]
        remote(land, land, x_send.at[j], x_recv.at[j], (row, partner(j))).wait_recv()
        return carry

    load_w.wait()
    rows_w, cols_w = depth // BLOCK, width // BLOCK

    def mask_rows(i, carry):
        at = pl.ds(pl.multiple_of(i * BLOCK, BLOCK), BLOCK)
        for j in range(cols_w):
            to = pl.ds(j * BLOCK, BLOCK)
            keep = mask_smem[i, j].astype(F32)
            W[at, to] = (W[at, to].astype(F32) * keep).astype(BF16)
        return carry

    lax.fori_loop(0, rows_w, mask_rows, 0)

    def flip(j, carry):
        at = pl.ds(pl.multiple_of(j * 256, 256), 256)
        WT[at, :] = W[:, at].T
        return carry

    lax.fori_loop(0, width // 256, flip, 0)

    def gather_step(dist):
        for part in range(2):
            for way in (UP, DOWN):
                if dist > last(way, part):
                    continue
                gather_copy(way, part, dist - 1).wait_recv()
                if dist < last(way, part):
                    gather_copy(way, part, dist).start()
                rel = (-dist if way == UP else dist) % NZ
                share_copy(rel, part).start()

    def grad_partial(rel):
        share_wait(rel)
        value = jnp.dot(C[pl.ds(rel * 2 * tok, 2 * tok), :], WT[...], preferred_element_type=F32).astype(BF16)
        there = 2 * ((z + rel) % NZ)
        for owner in range(2):
            dest = there + owner
            G[rel, owner] = value[owner * tok:(owner + 1) * tok]

            @pl.when(dest == col)
            def _():
                GR[dest] = G[rel, owner]

            @pl.when(dest != col)
            def _():
                remote(G.at[rel, owner], GR.at[col], g_send.at[rel, owner], g_recv.at[col], (row, dest)).start()

    def product(rel, carry):
        there = (z + rel) % NZ
        x_pair = X[pl.ds(2 * there, 2)].reshape(2 * tok, depth)
        XT[:, pl.ds(pl.multiple_of(rel * 2 * tok, 2 * tok), 2 * tok)] = x_pair.T

        def column(n, carry):
            at = pl.ds(pl.multiple_of(n * 256, 256), 256)
            value = jnp.dot(x_pair, W[:, at], preferred_element_type=F32)
            first, second = value[:tok], value[tok:]
            PO[rel, :, at] = jnp.where(core == 0, first, second)
            PS_out[rel, :, at] = jnp.where(core == 0, second, first).astype(BF16)
            return carry

        lax.fori_loop(0, width // 256, column, 0)
        pair_copy(rel).start()
        return carry

    def pair_copy(rel):
        return remote(PS_out.at[rel], PS.at[rel], ps_send.at[rel], ps_recv.at[rel], sibling)

    def reduce_copy(way, part, dist):
        return remote(S.at[way, part, dist], R.at[way, part, dist], r_send.at[way, part, dist], r_recv.at[way, part, dist], toward[way])

    def reduce_send(way, part, dist):
        rel = (dist if way == UP else -dist) % NZ
        at = pl.ds(part * half, half)
        total = PO[rel, at, :] + PS[rel, at, :].astype(F32)
        if dist < last(way, part):
            reduce_copy(way, part, dist + 1).wait_recv()
            total += R[way, part, dist + 1].astype(F32)
        S[way, part, dist] = total.astype(BF16)
        reduce_copy(way, part, dist).start()

    def reduce_step(step):
        for way in (UP, DOWN):
            for part in (way, 1 - way):
                dist = last(way, part) - step
                if dist >= 1:
                    reduce_send(way, part, dist)

    gather_step(1)
    grad_partial(0)
    gather_step(2)
    grad_partial(1)
    grad_partial(NZ - 1)
    gather_step(3)
    lax.fori_loop(1, NC, x_wait, 0)
    lax.fori_loop(0, NZ, product, 0)
    gather_step(4)
    for rel in range(NZ):
        pair_copy(rel).wait_recv()
    reduce_step(0)
    for rel in (2, 3, 4, 5, 6):
        grad_partial(rel)
    reduce_step(1)

    def weight_grad(n, carry):
        at = pl.ds(pl.multiple_of(n * 256, 256), 256)
        value = jnp.dot(XT[...], C[:, at], preferred_element_type=F32)
        for i in range(rows_w):
            for j in range(2):
                keep = mask_smem[i, n * 2 + j].astype(F32) * scale
                piece = value[i * BLOCK:(i + 1) * BLOCK, j * BLOCK:(j + 1) * BLOCK] * keep
                WG[pl.ds(i * BLOCK, BLOCK), pl.ds(pl.multiple_of(n * 256 + j * BLOCK, BLOCK), BLOCK)] = piece.astype(BF16)
        return carry

    lax.fori_loop(0, width // 256, weight_grad, 0)
    store_wg = pltpu.make_async_copy(WG, wg_hbm, store_sem.at[0])
    store_wg.start()
    reduce_step(2)

    def g_wait(j, carry):
        other = (col + j) % NC
        remote(GR.at[other], GR.at[other], g_send.at[0, 0], g_recv.at[other], (row, other)).wait_recv()
        return carry

    lax.fori_loop(1, NC, g_wait, 0)

    def g_sum(i, carry):
        at = pl.ds(pl.multiple_of(i * 16, 16), 16)
        total = GR[0, at, :].astype(F32)
        for c in range(1, NC):
            total += GR[c, at, :].astype(F32)
        IG[at, :] = total.astype(BF16)
        return carry

    lax.fori_loop(0, tok // 16, g_sum, 0)
    store_ig = pltpu.make_async_copy(IG, ig_hbm, store_sem.at[1])
    store_ig.start()
    reduce_step(3)

    for part in range(2):
        for way in (UP, DOWN):
            reduce_copy(way, part, 1).wait_recv()
        at = pl.ds(part * half, half)
        total = PO[0, at, :] + PS[0, at, :].astype(F32)
        total += R[UP, part, 1].astype(F32) + R[DOWN, part, 1].astype(F32)
        OUT[at, :] = total.astype(BF16)
    store_out = pltpu.make_async_copy(OUT, out_hbm, store_sem.at[2])
    store_out.start()

    for part in range(2):
        for way in (UP, DOWN):
            for dist in range(last(way, part)):
                gather_copy(way, part, dist).wait_send()
                reduce_copy(way, part, dist + 1).wait_send()
        for rel in range(NZ):
            share_copy(rel, part).wait_send()
    for rel in range(NZ):
        pair_copy(rel).wait_send()
        for owner in range(2):
            dest = 2 * ((z + rel) % NZ) + owner

            @pl.when(dest != col)
            def _():
                remote(G.at[rel, owner], GR.at[col], g_send.at[rel, owner], g_recv.at[col], (row, dest)).wait_send()

    def x_sent(j, carry):
        x_copy(j).wait_send()
        return carry

    lax.fori_loop(1, NC, x_sent, 0)
    store_wg.wait()
    store_ig.wait()
    store_out.wait()


def local(inputs, weight, mask, cotangent):
    tok, depth = inputs.shape
    width = weight.shape[1]
    half = tok // 2
    steps = NZ // 2 + 1
    dma = pltpu.SemaphoreType.DMA
    hbm = pl.BlockSpec(memory_space=pl.ANY)
    tokens = tok * NC
    return pl.pallas_call(
        functools.partial(kernel, float(tokens) ** -0.5),
        out_shape=(
            jax.ShapeDtypeStruct((tok, width), BF16),
            jax.ShapeDtypeStruct((tok, depth), BF16),
            jax.ShapeDtypeStruct((depth, width), BF16),
        ),
        in_specs=[hbm, hbm, pl.BlockSpec(memory_space=pltpu.SMEM), hbm],
        out_specs=(hbm, hbm, hbm),
        scratch_shapes=[
            pltpu.VMEM((NC, tok, depth), BF16),
            pltpu.VMEM((depth, tokens), BF16),
            pltpu.VMEM((depth, width), BF16),
            pltpu.VMEM((width, depth), BF16),
            pltpu.VMEM((tokens, width), BF16),
            pltpu.VMEM((NZ, tok, width), F32),
            pltpu.VMEM((NZ, tok, width), BF16),
            pltpu.VMEM((NZ, tok, width), BF16),
            pltpu.VMEM((2, 2, steps, half, width), BF16),
            pltpu.VMEM((2, 2, steps, half, width), BF16),
            pltpu.VMEM((NZ, 2, tok, depth), BF16),
            pltpu.VMEM((NC, tok, depth), BF16),
            pltpu.VMEM((depth, width), BF16),
            pltpu.VMEM((tok, width), BF16),
            pltpu.VMEM((tok, depth), BF16),
            dma((3,)),
            dma((NC,)), dma((NC,)),
            dma((2, 2, steps)), dma((2, 2, steps)),
            dma((NZ, 2)), dma((NZ, 2)),
            dma((NZ,)), dma((NZ,)),
            dma((2, 2, steps)), dma((2, 2, steps)),
            dma((NZ, 2)), dma((NC,)),
            dma((3,)),
        ],
        compiler_params=pltpu.CompilerParams(
            collective_id=0, has_side_effects=True, vmem_limit_bytes=60 * 1024 * 1024
        ),
        cost_estimate=pl.CostEstimate(
            flops=6 * tokens * depth * width, bytes_accessed=4 * depth * width + 4 * tok * (width + depth), transcendentals=0
        ),
    )(inputs, weight, mask, cotangent)


def solution(mesh):
    placed = (P("col", "row"), P("row", "col"), P("row", "col"), P("row", "col"))
    return jax.shard_map(
        local,
        mesh=mesh,
        in_specs=placed,
        out_specs=(P("row", "col"), P("col", "row"), P("row", "col")),
        check_vma=False,
    )
```

time: 276 us -> 117 us (0.42); the launches traced: 273 us -> 117 us
  waiting for transfers between devices: 208 us -> 0 us
  Pallas kernels: 0 us -> 110 us
  matrix products: 27.3 us -> 0 us
  local copies, waits for them, and re-layouts: 22.8 us -> 6.23 us
  between operations: 13.8 us -> 0.64 us
    unnamed x6 -> x0, waiting for transfers between devices: 121 us -> none
    pallas_call x0 -> x1, Pallas kernels: none -> 110 us  [local(): pl.pallas_call(functools.partial(kernel, float(tokens) ** (-0.5)), out_sh...]
    all_gather x2 -> x0, waiting for transfers between devices: 87.6 us -> none  [the longest x1 51.7 us: local(): shard_rows = lax.all_gather(cotangent, 'row', axis=0, tiled=True)]
    dot_general x3 -> x0, matrix products: 27.3 us -> none  [the longest x1 9.14 us: local(): lax.dot_general(chosen, shard_rows, (((0,), (0,)), ((), ())), preferred_e...]
    unnamed x4 -> x3, local copies, waits for them, and re-layouts: 19.4 us -> 6.23 us
    reshape x1 -> x0, local copies, waits for them, and re-layouts: 2.78 us -> none  [expand_mask(): return widened.reshape(tile_rows * BLOCK, tile_cols * BLOCK)]
  transfers between devices with their start and end apart: 4 -> 0, of which waited for: 4 -> 0; matrix products, arithmetic and copies ran while one was open for 19% -> 0% of each run, Pallas kernels for 0% -> 0%
where the time goes in v1:
time: 117 us
  Pallas kernels  110 us (94%)
  local copies, waits for them, and re-layouts  6.23 us (5%)
    pallas_call x1, Pallas kernels, local(): pl.pallas_call(functools.partial(kernel, float(tokens) ** (-0.5)), out_sh...  110 us
    unnamed x3, local copies, waits for them, and re-layouts  6.23 us

profile of v1, /device:TPU:1, one launch (start us, length us, event | category | flops | bytes accessed | tf_op | source)
XLA Modules:
  0.0 117.1 jit_solution(17087227391021364771)
XLA Ops:
  0.6 110.2 %shard_map.67 = (bf16[128,1792]{1,0:T(8,128)(2,1)}, bf16[128,512]{1,0:T(8,128)(2,1)}, bf16[512,1792]{1,0:T(8,128)(2,1)}) custom-call(bf16[128,512]{1,0:T(8,128)(2,1)} %x_hbm.1, bf16[512,1792]{1,0:T(8,128)(2,1)} %w_hbm.1, s32[4,14]{1,0:T(4,128)} %mask_smem.1, bf16[128,1792]{1,0:T(8,128)(2,1)} %c_hbm.1), custom_call_target="tpu_custom_call" | custom-call | flops 11274289152 | bytes 4849664 | tf_op jit(solution)/shard_map/pallas_call | solution.py:298
  110.9 1.8 %copy.10 = bf16[128,1792]{1,0:T(8,128)(2,1)} copy(bf16[128,1792]{1,0:T(8,128)(2,1)} %get-tuple-element.6) | data formatting | bytes 917504
  112.7 1.6 %copy.11 = bf16[128,512]{1,0:T(8,128)(2,1)} copy(bf16[128,512]{1,0:T(8,128)(2,1)} %get-tuple-element.7) | data formatting | bytes 262144
  114.2 2.8 %copy.12 = bf16[512,1792]{1,0:T(8,128)(2,1)} copy(bf16[512,1792]{1,0:T(8,128)(2,1)} %get-tuple-element.8) | data formatting | bytes 3670016

commit v2 on v1

--- a/solution.py
+++ b/solution.py
@@ -46,16 +46,16 @@
     toward = (up, down)
     my_rows = core * tok
 
-    def partner(j):
-        xx, yy = col % 4, col // 4
-        return ((yy + j // 4) % 4) * 4 + (xx + j % 4) % 4
-
-    def sender(j):
-        xx, yy = col % 4, col // 4
-        return ((yy + 4 - j // 4) % 4) * 4 + (xx + 4 - j % 4) % 4
+    cx, cy = col % 4, col // 4
+
+    def step_x(n):
+        return (row, cy * 4 + (cx + n + 4) % 4)
+
+    def step_y(n):
+        return (row, ((cy + n + 4) % 4) * 4 + cx)
 
     load_c = pltpu.make_async_copy(c_hbm, C.at[pl.ds(my_rows, tok)], load_sem.at[0])
-    load_x = pltpu.make_async_copy(x_hbm, X.at[col], load_sem.at[1])
+    load_x = pltpu.make_async_copy(x_hbm, X.at[cy, cx], load_sem.at[1])
     load_w = pltpu.make_async_copy(w_hbm, W, load_sem.at[2])
     load_c.start()
     load_x.start()
@@ -66,7 +66,7 @@
         pl.semaphore_signal(barrier, inc=1, device_id=device, device_id_type=pl.DeviceIdType.MESH)
 
     def greet(j, carry):
-        pl.semaphore_signal(barrier, inc=1, device_id=(row, partner(j)), device_id_type=pl.DeviceIdType.MESH)
+        pl.semaphore_signal(barrier, inc=1, device_id=(row, (col + j) % NC), device_id_type=pl.DeviceIdType.MESH)
         return carry
 
     lax.fori_loop(1, NC, greet, 0)
@@ -91,27 +91,45 @@
     def last(way, part):
         return NZ // 2 if part == way else NZ // 2 - 1
 
+    quarter = half // 2
+
+    def x_copy(h, stage, way):
+        sign = 1 if way == UP else -1
+        step = (step_x if (h == 0) == (stage < 2) else step_y)(sign)
+        back = 0 if stage % 2 == 0 else -sign
+        rows = pl.ds(h * half, half) if stage % 2 == 0 else pl.ds(h * half + way * quarter, quarter)
+        if stage < 2:
+            xs, ys = ((cx + back + 4) % 4, cy) if h == 0 else (cx, (cy + back + 4) % 4)
+            block = X.at[ys, xs, rows]
+        elif h == 0:
+            block = X.at[(cy + back + 4) % 4, :, rows]
+        else:
+            block = X.at[:, (cx + back + 4) % 4, rows]
+        return remote(block, block, x_send.at[h, stage, way], x_recv.at[h, stage, way], step)
+
+    def x_stage(stage):
+        for h in range(2):
+            for way in (UP, DOWN):
+                if stage % 2 == 1:
+                    x_copy(h, stage - 1, way).wait_recv()
+                    x_copy(h, stage, way).start()
+            if stage % 2 == 0:
+                for way in (UP, DOWN):
+                    if stage:
+                        x_copy(h, stage - 1, way).wait_recv()
+                for way in (UP, DOWN):
+                    if stage < 4:
+                        x_copy(h, stage, way).start()
+
     load_c.wait()
-    for part in range(2):
-        for way in (UP, DOWN):
-            gather_copy(way, part, 0).start()
+    for way in (UP, DOWN):
+        gather_copy(way, 0, 0).start()
+    load_x.wait()
+    x_stage(0)
+    for way in (UP, DOWN):
+        gather_copy(way, 1, 0).start()
     for part in range(2):
         share_copy(0, part).start()
-    load_x.wait()
-
-    def x_copy(j):
-        return remote(X.at[col], X.at[col], x_send.at[j], x_recv.at[j], (row, partner(j)))
-
-    def x_start(j, carry):
-        x_copy(j).start()
-        return carry
-
-    lax.fori_loop(1, NC, x_start, 0)
-
-    def x_wait(j, carry):
-        land = X.at[sender(j)]
-        remote(land, land, x_send.at[j], x_recv.at[j], (row, partner(j))).wait_recv()
-        return carry
 
     load_w.wait()
     rows_w, cols_w = depth // BLOCK, width // BLOCK
@@ -133,16 +151,14 @@
 
     lax.fori_loop(0, width // 256, flip, 0)
 
-    def gather_step(dist):
-        for part in range(2):
-            for way in (UP, DOWN):
-                if dist > last(way, part):
-                    continue
-                gather_copy(way, part, dist - 1).wait_recv()
-                if dist < last(way, part):
-                    gather_copy(way, part, dist).start()
-                rel = (-dist if way == UP else dist) % NZ
-                share_copy(rel, part).start()
+    def gather_step(dist, lead):
+        for way in (UP, DOWN):
+            part = way if lead else 1 - way
+            gather_copy(way, part, dist - 1).wait_recv()
+            if dist < last(way, part):
+                gather_copy(way, part, dist).start()
+            rel = (-dist if way == UP else dist) % NZ
+            share_copy(rel, part).start()
 
     def grad_partial(rel):
         share_wait(rel)
@@ -160,10 +176,10 @@
             def _():
                 remote(G.at[rel, owner], GR.at[col], g_send.at[rel, owner], g_recv.at[col], (row, dest)).start()
 
-    def product(rel, carry):
+    def product(rel):
         there = (z + rel) % NZ
-        x_pair = X[pl.ds(2 * there, 2)].reshape(2 * tok, depth)
-        XT[:, pl.ds(pl.multiple_of(rel * 2 * tok, 2 * tok), 2 * tok)] = x_pair.T
+        x_pair = X[there // 2, pl.ds(2 * (there % 2), 2)].reshape(2 * tok, depth)
+        XT[:, pl.ds(rel * 2 * tok, 2 * tok)] = x_pair.T
 
         def column(n, carry):
             at = pl.ds(pl.multiple_of(n * 256, 256), 256)
@@ -175,7 +191,6 @@
 
         lax.fori_loop(0, width // 256, column, 0)
         pair_copy(rel).start()
-        return carry
 
     def pair_copy(rel):
         return remote(PS_out.at[rel], PS.at[rel], ps_send.at[rel], ps_recv.at[rel], sibling)
@@ -193,28 +208,10 @@
         S[way, part, dist] = total.astype(BF16)
         reduce_copy(way, part, dist).start()
 
-    def reduce_step(step):
+    def reduce_step(step, lead):
         for way in (UP, DOWN):
-            for part in (way, 1 - way):
-                dist = last(way, part) - step
-                if dist >= 1:
-                    reduce_send(way, part, dist)
-
-    gather_step(1)
-    grad_partial(0)
-    gather_step(2)
-    grad_partial(1)
-    grad_partial(NZ - 1)
-    gather_step(3)
-    lax.fori_loop(1, NC, x_wait, 0)
-    lax.fori_loop(0, NZ, product, 0)
-    gather_step(4)
-    for rel in range(NZ):
-        pair_copy(rel).wait_recv()
-    reduce_step(0)
-    for rel in (2, 3, 4, 5, 6):
-        grad_partial(rel)
-    reduce_step(1)
+            part = way if lead else 1 - way
+            reduce_send(way, part, last(way, part) - step)
 
     def weight_grad(n, carry):
         at = pl.ds(pl.multiple_of(n * 256, 256), 256)
@@ -226,10 +223,48 @@
                 WG[pl.ds(i * BLOCK, BLOCK), pl.ds(pl.multiple_of(n * 256 + j * BLOCK, BLOCK), BLOCK)] = piece.astype(BF16)
         return carry
 
-    lax.fori_loop(0, width // 256, weight_grad, 0)
+    x_stage(1)
+    grad_partial(0)
+    x_stage(2)
+    gather_step(1, True)
+    gather_step(1, False)
+    x_stage(3)
+    grad_partial(1)
+    grad_partial(7)
+    gather_step(2, True)
+    x_stage(4)
+    for rel in (4, 3, 5):
+        product(rel)
+    gather_step(2, False)
+    for rel in (2, 6):
+        product(rel)
+    grad_partial(2)
+    grad_partial(6)
+    gather_step(3, True)
+    for rel in (1, 7, 0):
+        product(rel)
+    for rel in (4, 3, 5):
+        pair_copy(rel).wait_recv()
+    reduce_step(0, True)
+    reduce_step(0, False)
+    gather_step(3, False)
+    grad_partial(3)
+    grad_partial(5)
+    gather_step(4, True)
+    grad_partial(4)
+    for rel in (2, 6, 1, 7, 0):
+        pair_copy(rel).wait_recv()
+    reduce_step(1, True)
+    lax.fori_loop(0, 2, weight_grad, 0)
+    reduce_step(1, False)
+    lax.fori_loop(2, 4, weight_grad, 0)
+    reduce_step(2, True)
+    lax.fori_loop(4, 6, weight_grad, 0)
+    reduce_step(2, False)
+    lax.fori_loop(6, width // 256, weight_grad, 0)
     store_wg = pltpu.make_async_copy(WG, wg_hbm, store_sem.at[0])
     store_wg.start()
-    reduce_step(2)
+    reduce_step(3, True)
 
     def g_wait(j, carry):
         other = (col + j) % NC
@@ -249,7 +284,6 @@
     lax.fori_loop(0, tok // 16, g_sum, 0)
     store_ig = pltpu.make_async_copy(IG, ig_hbm, store_sem.at[1])
     store_ig.start()
-    reduce_step(3)
 
     for part in range(2):
         for way in (UP, DOWN):
@@ -277,14 +311,28 @@
             def _():
                 remote(G.at[rel, owner], GR.at[col], g_send.at[rel, owner], g_recv.at[col], (row, dest)).wait_send()
 
-    def x_sent(j, carry):
-        x_copy(j).wait_send()
-        return carry
-
-    lax.fori_loop(1, NC, x_sent, 0)
+    for h in range(2):
+        for stage in range(4):
+            for way in (UP, DOWN):
+                x_copy(h, stage, way).wait_send()
     store_wg.wait()
     store_ig.wait()
     store_out.wait()
+
+
+def finish(out_in, ig_in, wg_in, out_hbm, ig_hbm, wg_hbm, OUT, IG, WG, sem):
+    rows = WG.shape[0] // 4
+    moves = [(wg_in.at[pl.ds(i * rows, rows)], WG.at[pl.ds(i * rows, rows)], wg_hbm.at[pl.ds(i * rows, rows)]) for i in range(4)]
+    moves += [(out_in, OUT, out_hbm), (ig_in, IG, ig_hbm)]
+    loads = [pltpu.make_async_copy(a, b, sem.at[0, i]) for i, (a, b, _) in enumerate(moves)]
+    stores = [pltpu.make_async_copy(b, c, sem.at[1, i]) for i, (_, b, c) in enumerate(moves)]
+    for load in loads:
+        load.start()
+    for load, store in zip(loads, stores):
+        load.wait()
+        store.start()
+    for store in stores:
+        store.wait()
 
 
 def local(inputs, weight, mask, cotangent):
@@ -295,7 +343,7 @@
     dma = pltpu.SemaphoreType.DMA
     hbm = pl.BlockSpec(memory_space=pl.ANY)
     tokens = tok * NC
-    return pl.pallas_call(
+    results = pl.pallas_call(
         functools.partial(kernel, float(tokens) ** -0.5),
         out_shape=(
             jax.ShapeDtypeStruct((tok, width), BF16),
@@ -305,7 +353,7 @@
         in_specs=[hbm, hbm, pl.BlockSpec(memory_space=pltpu.SMEM), hbm],
         out_specs=(hbm, hbm, hbm),
         scratch_shapes=[
-            pltpu.VMEM((NC, tok, depth), BF16),
+            pltpu.VMEM((4, 4, tok, depth), BF16),
             pltpu.VMEM((depth, tokens), BF16),
             pltpu.VMEM((depth, width), BF16),
             pltpu.VMEM((width, depth), BF16),
@@ -321,7 +369,7 @@
             pltpu.VMEM((tok, width), BF16),
             pltpu.VMEM((tok, depth), BF16),
             dma((3,)),
-            dma((NC,)), dma((NC,)),
+            dma((2, 4, 2)), dma((2, 4, 2)),
             dma((2, 2, steps)), dma((2, 2, steps)),
             dma((NZ, 2)), dma((NZ, 2)),
             dma((NZ,)), dma((NZ,)),
@@ -336,6 +384,14 @@
             flops=6 * tokens * depth * width, bytes_accessed=4 * depth * width + 4 * tok * (width + depth), transcendentals=0
         ),
     )(inputs, weight, mask, cotangent)
+    return pl.pallas_call(
+        finish,
+        out_shape=tuple(jax.ShapeDtypeStruct(r.shape, r.dtype) for r in results),
+        in_specs=[hbm] * 3,
+        out_specs=(hbm,) * 3,
+        scratch_shapes=[pltpu.VMEM(r.shape, r.dtype) for r in results] + [dma((2, 6))],
+        compiler_params=pltpu.CompilerParams(vmem_limit_bytes=60 * 1024 * 1024),
+    )(*results)
 
 
 def solution(mesh):

time: 117 us -> 112 us (0.957)
  the two profiles are of different devices: /device:TPU:1 before, /device:TPU:24 now
where the time goes in v2:
time: 112 us
  Pallas kernels  112 us (100%)
    pallas_call x1, Pallas kernels, local(): pl.pallas_call(functools.partial(kernel, float(tokens) ** (-0.5)), out_sh...  109 us
    pallas_call x1, Pallas kernels, local(): pl.pallas_call(finish, out_shape=tuple((jax.ShapeDtypeStruct(r.shape, r.d...  2.53 us

profile of v2, /device:TPU:24, one launch (start us, length us, event | category | flops | bytes accessed | tf_op | source)
XLA Modules:
  0.0 112.3 jit_solution(15015461168297928425)
XLA Ops:
  0.6 109.2 %shard_map.67 = (bf16[128,1792]{1,0:T(8,128)(2,1)}, bf16[128,512]{1,0:T(8,128)(2,1)}, bf16[512,1792]{1,0:T(8,128)(2,1)}) custom-call(bf16[128,512]{1,0:T(8,128)(2,1)} %x_hbm.1, bf16[512,1792]{1,0:T(8,128)(2,1)} %w_hbm.1, s32[4,14]{1,0:T(4,128)} %mask_smem.1, bf16[128,1792]{1,0:T(8,128)(2,1)} %c_hbm.1), custom_call_target="tpu_custom_call" | custom-call | flops 11274289152 | bytes 4849664 | tf_op jit(solution)/shard_map/pallas_call | solution.py:346
  109.8 2.5 %shard_map.68 = (bf16[128,1792]{1,0:T(8,128)(2,1)}, bf16[128,512]{1,0:T(8,128)(2,1)}, bf16[512,1792]{1,0:T(8,128)(2,1)}) custom-call(bf16[128,1792]{1,0:T(8,128)(2,1)} %get-tuple-element.6.out_in, bf16[128,512]{1,0:T(8,128)(2,1)} %get-tuple-element.7.ig_in, bf16[512,1792]{1,0:T(8,128)(2,1)} %get-tuple-element.8.wg_in), custom_call_target="tpu_custom_call" | custom-call | tf_op jit(solution)/shard_map/pallas_call | solution.py:387

commit v3 on v2

--- a/solution.py
+++ b/solution.py
@@ -224,22 +224,20 @@
         return carry
 
     x_stage(1)
-    grad_partial(0)
     x_stage(2)
     gather_step(1, True)
     gather_step(1, False)
     x_stage(3)
-    grad_partial(1)
-    grad_partial(7)
     gather_step(2, True)
     x_stage(4)
     for rel in (4, 3, 5):
         product(rel)
+    grad_partial(0)
     gather_step(2, False)
     for rel in (2, 6):
         product(rel)
-    grad_partial(2)
-    grad_partial(6)
+    grad_partial(1)
+    grad_partial(7)
     gather_step(3, True)
     for rel in (1, 7, 0):
         product(rel)
@@ -247,6 +245,8 @@
         pair_copy(rel).wait_recv()
     reduce_step(0, True)
     reduce_step(0, False)
+    grad_partial(2)
+    grad_partial(6)
     gather_step(3, False)
     grad_partial(3)
     grad_partial(5)

time: 112 us -> 87.7 us (0.78)
  the two profiles are of different devices: /device:TPU:24 before, /device:TPU:1 now
where the time goes in v3:
time: 87.7 us; the launch traced here: 87.6 us
  Pallas kernels  87 us (99%)
    pallas_call x1, Pallas kernels, local(): pl.pallas_call(functools.partial(kernel, float(tokens) ** (-0.5)), out_sh...  84.4 us
    pallas_call x1, Pallas kernels, local(): pl.pallas_call(finish, out_shape=tuple((jax.ShapeDtypeStruct(r.shape, r.d...  2.53 us

profile of v3, /device:TPU:1, one launch (start us, length us, event | category | flops | bytes accessed | tf_op | source)
XLA Modules:
  0.0 87.6 jit_solution(16932153341540108628)
XLA Ops:
  0.6 84.4 %shard_map.67 = (bf16[128,1792]{1,0:T(8,128)(2,1)}, bf16[128,512]{1,0:T(8,128)(2,1)}, bf16[512,1792]{1,0:T(8,128)(2,1)}) custom-call(bf16[128,512]{1,0:T(8,128)(2,1)} %x_hbm.1, bf16[512,1792]{1,0:T(8,128)(2,1)} %w_hbm.1, s32[4,14]{1,0:T(4,128)} %mask_smem.1, bf16[128,1792]{1,0:T(8,128)(2,1)} %c_hbm.1), custom_call_target="tpu_custom_call" | custom-call | flops 11274289152 | bytes 4849664 | tf_op jit(solution)/shard_map/pallas_call | solution.py:346
  85.1 2.5 %shard_map.68 = (bf16[128,1792]{1,0:T(8,128)(2,1)}, bf16[128,512]{1,0:T(8,128)(2,1)}, bf16[512,1792]{1,0:T(8,128)(2,1)}) custom-call(bf16[128,1792]{1,0:T(8,128)(2,1)} %get-tuple-element.6.out_in, bf16[128,512]{1,0:T(8,128)(2,1)} %get-tuple-element.7.ig_in, bf16[512,1792]{1,0:T(8,128)(2,1)} %get-tuple-element.8.wg_in), custom_call_target="tpu_custom_call" | custom-call | tf_op jit(solution)/shard_map/pallas_call | solution.py:387

commit v4 on v3

--- a/solution.py
+++ b/solution.py
@@ -62,15 +62,10 @@
     load_w.start()
 
     barrier = pltpu.get_barrier_semaphore()
-    for device in (up, down, sibling):
+    neighbours = (up, down, sibling, step_x(1), step_x(-1), step_y(1), step_y(-1))
+    for device in neighbours:
         pl.semaphore_signal(barrier, inc=1, device_id=device, device_id_type=pl.DeviceIdType.MESH)
-
-    def greet(j, carry):
-        pl.semaphore_signal(barrier, inc=1, device_id=(row, (col + j) % NC), device_id_type=pl.DeviceIdType.MESH)
-        return carry
-
-    lax.fori_loop(1, NC, greet, 0)
-    pl.semaphore_wait(barrier, NC + 2)
+    pl.semaphore_wait(barrier, len(neighbours))
 
     def chunk(rel, part, owner=core):
         return C.at[pl.ds(rel * 2 * tok + owner * tok + part * half, half)]

time: 87.7 us -> 85.1 us (0.970); the launches traced: 87.6 us -> 83.9 us
  Pallas kernels: 87 us -> 83.2 us
    pallas_call x1, Pallas kernels: 84.4 us -> 80.7 us  [local(): pl.pallas_call(functools.partial(kernel, float(tokens) ** (-0.5)), out_sh...]
where the time goes in v4:
time: 85.1 us; the launch traced here: 83.9 us
  Pallas kernels  83.2 us (98%)
    pallas_call x1, Pallas kernels, local(): pl.pallas_call(functools.partial(kernel, float(tokens) ** (-0.5)), out_sh...  80.7 us
    pallas_call x1, Pallas kernels, local(): pl.pallas_call(finish, out_shape=tuple((jax.ShapeDtypeStruct(r.shape, r.d...  2.53 us

profile of v4, /device:TPU:1, one launch (start us, length us, event | category | flops | bytes accessed | tf_op | source)
XLA Modules:
  0.0 83.9 jit_solution(7374264095002127370)
XLA Ops:
  0.6 80.7 %shard_map.67 = (bf16[128,1792]{1,0:T(8,128)(2,1)}, bf16[128,512]{1,0:T(8,128)(2,1)}, bf16[512,1792]{1,0:T(8,128)(2,1)}) custom-call(bf16[128,512]{1,0:T(8,128)(2,1)} %x_hbm.1, bf16[512,1792]{1,0:T(8,128)(2,1)} %w_hbm.1, s32[4,14]{1,0:T(4,128)} %mask_smem.1, bf16[128,1792]{1,0:T(8,128)(2,1)} %c_hbm.1), custom_call_target="tpu_custom_call" | custom-call | flops 11274289152 | bytes 4849664 | tf_op jit(solution)/shard_map/pallas_call | solution.py:341
  81.3 2.5 %shard_map.68 = (bf16[128,1792]{1,0:T(8,128)(2,1)}, bf16[128,512]{1,0:T(8,128)(2,1)}, bf16[512,1792]{1,0:T(8,128)(2,1)}) custom-call(bf16[128,1792]{1,0:T(8,128)(2,1)} %get-tuple-element.6.out_in, bf16[128,512]{1,0:T(8,128)(2,1)} %get-tuple-element.7.ig_in, bf16[512,1792]{1,0:T(8,128)(2,1)} %get-tuple-element.8.wg_in), custom_call_target="tpu_custom_call" | custom-call | tf_op jit(solution)/shard_map/pallas_call | solution.py:382

commit v5 on v4

--- a/solution.py
+++ b/solution.py
@@ -28,9 +28,9 @@
 
 def kernel(
     scale,
-    x_hbm, w_hbm, mask_smem, c_hbm,
-    out_hbm, ig_hbm, wg_hbm,
-    X, XT, W, WT, C, PO, PS_out, PS, S, R, G, GR, WG, OUT, IG,
+    x_hbm, w_hbm, mask_hbm, c_hbm,
+    last_hbm, own_hbm, ig_hbm, wg_hbm,
+    mask_smem, X, XT, W, WT, C, PO, PS_out, PS, S, R, G, GR, WG, IG,
     load_sem, x_send, x_recv, az_send, az_recv, as_send, as_recv,
     ps_send, ps_recv, r_send, r_recv, g_send, g_recv, store_sem,
 ):
@@ -54,17 +54,20 @@
     def step_y(n):
         return (row, ((cy + n + 4) % 4) * 4 + cx)
 
+    barrier = pltpu.get_barrier_semaphore()
+    neighbours = (up, down, sibling, step_x(1), step_x(-1), step_y(1), step_y(-1))
+    for device in neighbours:
+        pl.semaphore_signal(barrier, inc=1, device_id=device, device_id_type=pl.DeviceIdType.MESH)
+
     load_c = pltpu.make_async_copy(c_hbm, C.at[pl.ds(my_rows, tok)], load_sem.at[0])
     load_x = pltpu.make_async_copy(x_hbm, X.at[cy, cx], load_sem.at[1])
     load_w = pltpu.make_async_copy(w_hbm, W, load_sem.at[2])
     load_c.start()
     load_x.start()
     load_w.start()
-
-    barrier = pltpu.get_barrier_semaphore()
-    neighbours = (up, down, sibling, step_x(1), step_x(-1), step_y(1), step_y(-1))
-    for device in neighbours:
-        pl.semaphore_signal(barrier, inc=1, device_id=device, device_id_type=pl.DeviceIdType.MESH)
+    load_mask = pltpu.make_async_copy(mask_hbm, mask_smem, load_sem.at[3])
+    load_mask.start()
+
     pl.semaphore_wait(barrier, len(neighbours))
 
     def chunk(rel, part, owner=core):
@@ -73,7 +76,8 @@
     def gather_copy(way, part, dist):
         rel = (-dist if way == UP else dist) % NZ
         land = (rel - 1 if way == UP else rel + 1) % NZ
-        return remote(chunk(rel, part), chunk(land, part), az_send.at[way, part, dist], az_recv.at[way, part, dist], toward[way])
+        src = c_hbm.at[pl.ds(part * half, half)] if dist == 0 else chunk(rel, part)
+        return remote(src, chunk(land, part), az_send.at[way, part, dist], az_recv.at[way, part, dist], toward[way])
 
     def share_copy(rel, part):
         return remote(chunk(rel, part), chunk(rel, part), as_send.at[rel, part], as_recv.at[rel, part], sibling)
@@ -100,7 +104,8 @@
             block = X.at[(cy + back + 4) % 4, :, rows]
         else:
             block = X.at[:, (cx + back + 4) % 4, rows]
-        return remote(block, block, x_send.at[h, stage, way], x_recv.at[h, stage, way], step)
+        src = x_hbm.at[rows] if stage == 0 else block
+        return remote(src, block, x_send.at[h, stage, way], x_recv.at[h, stage, way], step)
 
     def x_stage(stage):
         for h in range(2):
@@ -116,17 +121,18 @@
                     if stage < 4:
                         x_copy(h, stage, way).start()
 
-    load_c.wait()
     for way in (UP, DOWN):
         gather_copy(way, 0, 0).start()
-    load_x.wait()
     x_stage(0)
     for way in (UP, DOWN):
         gather_copy(way, 1, 0).start()
+    load_c.wait()
+    load_x.wait()
     for part in range(2):
         share_copy(0, part).start()
 
     load_w.wait()
+    load_mask.wait()
     rows_w, cols_w = depth // BLOCK, width // BLOCK
 
     def mask_rows(i, carry):
@@ -191,7 +197,8 @@
         return remote(PS_out.at[rel], PS.at[rel], ps_send.at[rel], ps_recv.at[rel], sibling)
 
     def reduce_copy(way, part, dist):
-        return remote(S.at[way, part, dist], R.at[way, part, dist], r_send.at[way, part, dist], r_recv.at[way, part, dist], toward[way])
+        land = last_hbm.at[way, pl.ds(part * half, half)] if dist == 1 else R.at[way, part, dist]
+        return remote(S.at[way, part, dist], land, r_send.at[way, part, dist], r_recv.at[way, part, dist], toward[way])
 
     def reduce_send(way, part, dist):
         rel = (dist if way == UP else -dist) % NZ
@@ -261,6 +268,10 @@
     store_wg.start()
     reduce_step(3, True)
 
+    PO[0] = PO[0] + PS[0].astype(F32)
+    store_own = pltpu.make_async_copy(PO.at[0], own_hbm, store_sem.at[2])
+    store_own.start()
+
     def g_wait(j, carry):
         other = (col + j) % NC
         remote(GR.at[other], GR.at[other], g_send.at[0, 0], g_recv.at[other], (row, other)).wait_recv()
@@ -282,19 +293,10 @@
 
     for part in range(2):
         for way in (UP, DOWN):
-            reduce_copy(way, part, 1).wait_recv()
-        at = pl.ds(part * half, half)
-        total = PO[0, at, :] + PS[0, at, :].astype(F32)
-        total += R[UP, part, 1].astype(F32) + R[DOWN, part, 1].astype(F32)
-        OUT[at, :] = total.astype(BF16)
-    store_out = pltpu.make_async_copy(OUT, out_hbm, store_sem.at[2])
-    store_out.start()
-
-    for part in range(2):
-        for way in (UP, DOWN):
             for dist in range(last(way, part)):
                 gather_copy(way, part, dist).wait_send()
-                reduce_copy(way, part, dist + 1).wait_send()
+                if dist:
+                    reduce_copy(way, part, dist + 1).wait_send()
         for rel in range(NZ):
             share_copy(rel, part).wait_send()
     for rel in range(NZ):
@@ -312,21 +314,26 @@
                 x_copy(h, stage, way).wait_send()
     store_wg.wait()
     store_ig.wait()
-    store_out.wait()
-
-
-def finish(out_in, ig_in, wg_in, out_hbm, ig_hbm, wg_hbm, OUT, IG, WG, sem):
-    rows = WG.shape[0] // 4
-    moves = [(wg_in.at[pl.ds(i * rows, rows)], WG.at[pl.ds(i * rows, rows)], wg_hbm.at[pl.ds(i * rows, rows)]) for i in range(4)]
-    moves += [(out_in, OUT, out_hbm), (ig_in, IG, ig_hbm)]
-    loads = [pltpu.make_async_copy(a, b, sem.at[0, i]) for i, (a, b, _) in enumerate(moves)]
-    stores = [pltpu.make_async_copy(b, c, sem.at[1, i]) for i, (_, b, c) in enumerate(moves)]
-    for load in loads:
-        load.start()
-    for load, store in zip(loads, stores):
-        load.wait()
-        store.start()
-    for store in stores:
+    store_own.wait()
+    for part in range(2):
+        for way in (UP, DOWN):
+            reduce_copy(way, part, 1).wait_recv()
+            reduce_copy(way, part, 1).wait_send()
+
+
+def finish(last, own, ig_in, wg_in, out_hbm, ig_hbm, wg_hbm, OUT, sem):
+    store_wg = pltpu.make_async_copy(wg_in, wg_hbm, sem.at[0])
+    store_ig = pltpu.make_async_copy(ig_in, ig_hbm, sem.at[1])
+    store_wg.start()
+    store_ig.start()
+    half = OUT.shape[0] // 2
+    stores = []
+    for part in range(2):
+        at = pl.ds(part * half, half)
+        OUT[at] = (own[at] + last[UP, at].astype(F32) + last[DOWN, at].astype(F32)).astype(BF16)
+        stores.append(pltpu.make_async_copy(OUT.at[at], out_hbm.at[at], sem.at[2 + part]))
+        stores[part].start()
+    for store in [store_wg, store_ig] + stores:
         store.wait()
 
 
@@ -341,13 +348,15 @@
     results = pl.pallas_call(
         functools.partial(kernel, float(tokens) ** -0.5),
         out_shape=(
-            jax.ShapeDtypeStruct((tok, width), BF16),
+            jax.ShapeDtypeStruct((2, tok, width), BF16),
+            jax.ShapeDtypeStruct((tok, width), F32),
             jax.ShapeDtypeStruct((tok, depth), BF16),
             jax.ShapeDtypeStruct((depth, width), BF16),
         ),
-        in_specs=[hbm, hbm, pl.BlockSpec(memory_space=pltpu.SMEM), hbm],
-        out_specs=(hbm, hbm, hbm),
+        in_specs=[hbm] * 4,
+        out_specs=(hbm,) * 4,
         scratch_shapes=[
+            pltpu.SMEM(mask.shape, mask.dtype),
             pltpu.VMEM((4, 4, tok, depth), BF16),
             pltpu.VMEM((depth, tokens), BF16),
             pltpu.VMEM((depth, width), BF16),
@@ -361,9 +370,8 @@
             pltpu.VMEM((NZ, 2, tok, depth), BF16),
             pltpu.VMEM((NC, tok, depth), BF16),
             pltpu.VMEM((depth, width), BF16),
-            pltpu.VMEM((tok, width), BF16),
             pltpu.VMEM((tok, depth), BF16),
-            dma((3,)),
+            dma((4,)),
             dma((2, 4, 2)), dma((2, 4, 2)),
             dma((2, 2, steps)), dma((2, 2, steps)),
             dma((NZ, 2)), dma((NZ, 2)),
@@ -373,19 +381,20 @@
             dma((3,)),
         ],
         compiler_params=pltpu.CompilerParams(
-            collective_id=0, has_side_effects=True, vmem_limit_bytes=60 * 1024 * 1024
+            collective_id=0, has_side_effects=True, vmem_limit_bytes=44 * 1024 * 1024
         ),
         cost_estimate=pl.CostEstimate(
             flops=6 * tokens * depth * width, bytes_accessed=4 * depth * width + 4 * tok * (width + depth), transcendentals=0
         ),
-    )(inputs, weight, mask, cotangent)
+    )(*(pltpu.with_memory_space_constraint(a, pltpu.HBM) for a in (inputs, weight, mask, cotangent)))
+    shapes = ((tok, width), (tok, depth), (depth, width))
     return pl.pallas_call(
         finish,
-        out_shape=tuple(jax.ShapeDtypeStruct(r.shape, r.dtype) for r in results),
-        in_specs=[hbm] * 3,
+        out_shape=tuple(jax.ShapeDtypeStruct(shape, BF16) for shape in shapes),
+        in_specs=[pl.BlockSpec(memory_space=pltpu.VMEM)] * 4,
         out_specs=(hbm,) * 3,
-        scratch_shapes=[pltpu.VMEM(r.shape, r.dtype) for r in results] + [dma((2, 6))],
-        compiler_params=pltpu.CompilerParams(vmem_limit_bytes=60 * 1024 * 1024),
+        scratch_shapes=[pltpu.VMEM((tok, width), BF16), dma((4,))],
+        compiler_params=pltpu.CompilerParams(vmem_limit_bytes=8 * 1024 * 1024),
     )(*results)
 
 

time: 85.1 us -> 82.5 us (0.969)
  Pallas kernels: 83.2 us -> 81.1 us
    pallas_call x1, Pallas kernels: 2.53 us -> 1.45 us  [local(): pl.pallas_call(finish, out_shape=tuple((jax.ShapeDtypeStruct(shape, BF16)...]
    pallas_call x1, Pallas kernels: 80.7 us -> 79.6 us  [local(): pl.pallas_call(functools.partial(kernel, float(tokens) ** (-0.5)), out_sh...]
where the time goes in v5:
time: 82.5 us; the launch traced here: 81.7 us
  Pallas kernels  81.1 us (98%)
    pallas_call x1, Pallas kernels, local(): pl.pallas_call(functools.partial(kernel, float(tokens) ** (-0.5)), out_sh...  79.6 us

profile of v5, /device:TPU:1, one launch (start us, length us, event | category | flops | bytes accessed | tf_op | source)
XLA Modules:
  0.0 81.7 jit_solution(11508920783112549550)
XLA Ops:
  0.6 79.6 %shard_map.67 = (bf16[2,128,1792]{2,1,0:T(8,128)(2,1)S(1)}, f32[128,1792]{1,0:T(8,128)S(1)}, bf16[128,512]{1,0:T(8,128)(2,1)S(1)}, bf16[512,1792]{1,0:T(8,128)(2,1)S(1)}) custom-call(bf16[128,512]{1,0:T(8,128)(2,1)} %x_hbm.1, bf16[512,1792]{1,0:T(8,128)(2,1)} %w_hbm.1, s32[4,14]{1,0:T(4,128)} %mask_hbm.1, bf16[128,1792]{1,0:T(8,128)(2,1)} %c_hbm.1), custom_call_target="tpu_custom_call" | custom-call | flops 11274289152 | bytes 4849664 | tf_op jit(solution)/shard_map/pallas_call | solution.py:348
  80.3 1.4 %shard_map.68 = (bf16[128,1792]{1,0:T(8,128)(2,1)}, bf16[128,512]{1,0:T(8,128)(2,1)}, bf16[512,1792]{1,0:T(8,128)(2,1)}) custom-call(bf16[2,128,1792]{2,1,0:T(8,128)(2,1)S(1)} %get-tuple-element.7.last, f32[128,1792]{1,0:T(8,128)S(1)} %get-tuple-element.8.own, bf16[128,512]{1,0:T(8,128)(2,1)S(1)} %get-tuple-element.9.ig_in, ...), custom_call_target="tpu_custom_call" | custom-call | tf_op jit(solution)/shard_map/pallas_call | solution.py:391

commit v6 on v5

--- a/solution.py
+++ b/solution.py
@@ -55,19 +55,14 @@
         return (row, ((cy + n + 4) % 4) * 4 + cx)
 
     barrier = pltpu.get_barrier_semaphore()
-    neighbours = (up, down, sibling, step_x(1), step_x(-1), step_y(1), step_y(-1))
+    neighbours = (step_x(1), step_x(-1), step_y(1), step_y(-1), up, down, sibling)
     for device in neighbours:
         pl.semaphore_signal(barrier, inc=1, device_id=device, device_id_type=pl.DeviceIdType.MESH)
 
     load_c = pltpu.make_async_copy(c_hbm, C.at[pl.ds(my_rows, tok)], load_sem.at[0])
     load_x = pltpu.make_async_copy(x_hbm, X.at[cy, cx], load_sem.at[1])
     load_w = pltpu.make_async_copy(w_hbm, W, load_sem.at[2])
-    load_c.start()
-    load_x.start()
-    load_w.start()
     load_mask = pltpu.make_async_copy(mask_hbm, mask_smem, load_sem.at[3])
-    load_mask.start()
-
     pl.semaphore_wait(barrier, len(neighbours))
 
     def chunk(rel, part, owner=core):
@@ -126,6 +121,8 @@
     x_stage(0)
     for way in (UP, DOWN):
         gather_copy(way, 1, 0).start()
+    for load in (load_c, load_x, load_w, load_mask):
+        load.start()
     load_c.wait()
     load_x.wait()
     for part in range(2):
@@ -322,18 +319,18 @@
 
 
 def finish(last, own, ig_in, wg_in, out_hbm, ig_hbm, wg_hbm, OUT, sem):
-    store_wg = pltpu.make_async_copy(wg_in, wg_hbm, sem.at[0])
-    store_ig = pltpu.make_async_copy(ig_in, ig_hbm, sem.at[1])
-    store_wg.start()
-    store_ig.start()
+    rows = wg_in.shape[0] // 4
+    stores = [pltpu.make_async_copy(wg_in.at[pl.ds(i * rows, rows)], wg_hbm.at[pl.ds(i * rows, rows)], sem.at[2 + i]) for i in range(4)]
+    stores.append(pltpu.make_async_copy(ig_in, ig_hbm, sem.at[6]))
+    for store in stores:
+        store.start()
     half = OUT.shape[0] // 2
-    stores = []
     for part in range(2):
         at = pl.ds(part * half, half)
         OUT[at] = (own[at] + last[UP, at].astype(F32) + last[DOWN, at].astype(F32)).astype(BF16)
-        stores.append(pltpu.make_async_copy(OUT.at[at], out_hbm.at[at], sem.at[2 + part]))
-        stores[part].start()
-    for store in [store_wg, store_ig] + stores:
+        stores.append(pltpu.make_async_copy(OUT.at[at], out_hbm.at[at], sem.at[part]))
+        stores[-1].start()
+    for store in stores:
         store.wait()
 
 
@@ -393,7 +390,7 @@
         out_shape=tuple(jax.ShapeDtypeStruct(shape, BF16) for shape in shapes),
         in_specs=[pl.BlockSpec(memory_space=pltpu.VMEM)] * 4,
         out_specs=(hbm,) * 3,
-        scratch_shapes=[pltpu.VMEM((tok, width), BF16), dma((4,))],
+        scratch_shapes=[pltpu.VMEM((tok, width), BF16), dma((7,))],
         compiler_params=pltpu.CompilerParams(vmem_limit_bytes=8 * 1024 * 1024),
     )(*results)
 

time: 82.5 us -> 82.5 us (level)
  no operation moved by 1% of the time
where the time goes in v6:
time: 82.5 us; the launch traced here: 81.7 us
  Pallas kernels  81.1 us (98%)
    pallas_call x1, Pallas kernels, local(): pl.pallas_call(functools.partial(kernel, float(tokens) ** (-0.5)), out_sh...  79.6 us

profile of v6, /device:TPU:1, one launch (start us, length us, event | category | flops | bytes accessed | tf_op | source)
XLA Modules:
  0.0 81.7 jit_solution(2027672873856847803)
XLA Ops:
  0.6 79.6 %shard_map.67 = (bf16[2,128,1792]{2,1,0:T(8,128)(2,1)S(1)}, f32[128,1792]{1,0:T(8,128)S(1)}, bf16[128,512]{1,0:T(8,128)(2,1)S(1)}, bf16[512,1792]{1,0:T(8,128)(2,1)S(1)}) custom-call(bf16[128,512]{1,0:T(8,128)(2,1)} %x_hbm.1, bf16[512,1792]{1,0:T(8,128)(2,1)} %w_hbm.1, s32[4,14]{1,0:T(4,128)} %mask_hbm.1, bf16[128,1792]{1,0:T(8,128)(2,1)} %c_hbm.1), custom_call_target="tpu_custom_call" | custom-call | flops 11274289152 | bytes 4849664 | tf_op jit(solution)/shard_map/pallas_call | solution.py:345
  80.3 1.5 %shard_map.68 = (bf16[128,1792]{1,0:T(8,128)(2,1)}, bf16[128,512]{1,0:T(8,128)(2,1)}, bf16[512,1792]{1,0:T(8,128)(2,1)}) custom-call(bf16[2,128,1792]{2,1,0:T(8,128)(2,1)S(1)} %get-tuple-element.7.last, f32[128,1792]{1,0:T(8,128)S(1)} %get-tuple-element.8.own, bf16[128,512]{1,0:T(8,128)(2,1)S(1)} %get-tuple-element.9.ig_in, ...), custom_call_target="tpu_custom_call" | custom-call | tf_op jit(solution)/shard_map/pallas_call | solution.py:388

commit v7 on v6

--- a/solution.py
+++ b/solution.py
@@ -116,9 +116,9 @@
                     if stage < 4:
                         x_copy(h, stage, way).start()
 
+    x_stage(0)
     for way in (UP, DOWN):
         gather_copy(way, 0, 0).start()
-    x_stage(0)
     for way in (UP, DOWN):
         gather_copy(way, 1, 0).start()
     for load in (load_c, load_x, load_w, load_mask):

time: 82.5 us -> 82.5 us (level)
  no operation moved by 1% of the time
where the time goes in v7:
time: 82.5 us; the launch traced here: 81.7 us
  Pallas kernels  81.1 us (98%)
    pallas_call x1, Pallas kernels, local(): pl.pallas_call(functools.partial(kernel, float(tokens) ** (-0.5)), out_sh...  79.6 us

profile of v7, /device:TPU:1, one launch (start us, length us, event | category | flops | bytes accessed | tf_op | source)
XLA Modules:
  0.0 81.7 jit_solution(33525716734276878)
XLA Ops:
  0.6 79.6 %shard_map.67 = (bf16[2,128,1792]{2,1,0:T(8,128)(2,1)S(1)}, f32[128,1792]{1,0:T(8,128)S(1)}, bf16[128,512]{1,0:T(8,128)(2,1)S(1)}, bf16[512,1792]{1,0:T(8,128)(2,1)S(1)}) custom-call(bf16[128,512]{1,0:T(8,128)(2,1)} %x_hbm.1, bf16[512,1792]{1,0:T(8,128)(2,1)} %w_hbm.1, s32[4,14]{1,0:T(4,128)} %mask_hbm.1, bf16[128,1792]{1,0:T(8,128)(2,1)} %c_hbm.1), custom_call_target="tpu_custom_call" | custom-call | flops 11274289152 | bytes 4849664 | tf_op jit(solution)/shard_map/pallas_call | solution.py:345
  80.3 1.5 %shard_map.68 = (bf16[128,1792]{1,0:T(8,128)(2,1)}, bf16[128,512]{1,0:T(8,128)(2,1)}, bf16[512,1792]{1,0:T(8,128)(2,1)}) custom-call(bf16[2,128,1792]{2,1,0:T(8,128)(2,1)S(1)} %get-tuple-element.7.last, f32[128,1792]{1,0:T(8,128)S(1)} %get-tuple-element.8.own, bf16[128,512]{1,0:T(8,128)(2,1)S(1)} %get-tuple-element.9.ig_in, ...), custom_call_target="tpu_custom_call" | custom-call | tf_op jit(solution)/shard_map/pallas_call | solution.py:388
